TPU v7x, 32 devices: a whole 2x2x4 slice. The times are simulated.
32 devices in a mesh: group: 2 (over x), tp: 16 (over z, y, core), pool: 1.
Axes of the slice: x: 2, y: 2, z: 4, core: 2. Of those that a mesh axis runs over, the one named last changes fastest.
Arguments:
- prompt_x: bfloat16 [2048, 8192], P(('group', 'pool'), 'tp'), parts along dimension 0, may hold values from -6 to 6
- decode_x: bfloat16 [4, 32, 8192], P(None, ('group', 'pool'), 'tp'), parts along dimension 1, may hold values from -240 to 240
- w_query: bfloat16 [8192, 8192], P(None, 'tp'), may hold values from -0.0625 to 0.0625
- w_keyval: bfloat16 [8192, 2048], P('tp'), may hold values from -0.0625 to 0.0625
- w_out: bfloat16 [8192, 8192], P('tp'), may hold values from -0.0625 to 0.0625
- prompt_blocks: int32 [32], P('group'), parts along dimension 0, may hold values from 1 to 32, 64 in all
- prompt_row: int32 [32], P('group'), parts along dimension 0, may hold values from 0 to 15, each once
Outputs:
- decode_out: bfloat16 [4, 32, 8192], P(None, ('group', 'pool'), 'tp'), parts along dimension 1
There are 2 independent parts, one for each index of `group`. A program takes and returns all parts, laid end to end along the dimension named above; an argument that names none is the same for every part. Nothing has to cross between parts.
Inputs may be any that keep to these rules, and one draw needn't show every extreme that they name: `prompt_blocks`: each prompt has at least one block, the prompts fill the span exactly, and one prompt has exactly 32 blocks. `prompt_row`: every decode row continues exactly one prompt.
All inputs are finite; a program needn't handle non-finite values. Where the computation divides by a largest or mean magnitude, that divisor is 1e-20 or more.
Results may differ from a plain program's by a relative error of at most 0.018.
Values may be sent and summed in bfloat16 or wider, within the bound.
No kernel may reach another device: no remote copies, remote signals or barrier semaphores. Data moves between devices by JAX's collectives and lax.ppermute only.
A program may use at most 128 MiB of HBM per device.

v0:
```python
import math
import jax
import jax.numpy as jnp
import numpy as np
from jax import lax
from jax.sharding import PartitionSpec as P

KVH = 8
HD = 128
BLK = 16


def block_rows(prompt_blocks, prompt_row, total_blocks):
    block_ends = jnp.cumsum(prompt_blocks)
    positions = jnp.arange(total_blocks, dtype=jnp.int32)
    owner_seq = jnp.sum((block_ends[None, :] <= positions[:, None]).astype(jnp.int32), axis=1)
    seq_match = owner_seq[:, None] == jnp.arange(prompt_row.shape[0], dtype=jnp.int32)[None, :]
    return jnp.sum(jnp.where(seq_match, prompt_row[None, :], 0), axis=1)


def attend(queries, cache_vals, cache_scale, slot_row, fresh_keyval, row_ids):
    head_dim = queries.shape[-1]
    inverse_root = 1.0 / math.sqrt(head_dim)
    query_f32 = queries.astype(jnp.float32)
    scale_f32 = cache_scale.astype(jnp.float32)
    cache_keys = cache_vals[:, :, :head_dim].astype(jnp.float32) * scale_f32[:, 0][:, None, None]
    cache_values = cache_vals[:, :, head_dim:].astype(jnp.float32) * scale_f32[:, 1][:, None, None]
    cache_score = jnp.einsum("srgd,nkd->srgnk", query_f32, cache_keys) * inverse_root
    visible = slot_row[None, :] == row_ids[:, None]
    cache_score = jnp.where(visible[None, :, None, :, None], cache_score, -jnp.inf)
    fresh_f32 = fresh_keyval.astype(jnp.float32)
    fresh_score = jnp.einsum("srgd,trd->srgt", query_f32, fresh_f32[:, :, :head_dim]) * inverse_root
    step_index = jnp.arange(queries.shape[0], dtype=jnp.int32)
    causal = step_index[:, None] >= step_index[None, :]
    fresh_score = jnp.where(causal[:, None, None, :], fresh_score, -jnp.inf)
    top_score = jnp.maximum(jnp.max(cache_score, axis=(3, 4)), jnp.max(fresh_score, axis=3))
    cache_weight = jnp.exp(cache_score - top_score[..., None, None])
    fresh_weight = jnp.exp(fresh_score - top_score[..., None])
    denominator = jnp.sum(cache_weight, axis=(3, 4)) + jnp.sum(fresh_weight, axis=3)
    weighted = jnp.einsum("srgnk,nkd->srgd", cache_weight, cache_values)
    weighted = weighted + jnp.einsum("srgt,trd->srgd", fresh_weight, fresh_f32[:, :, head_dim:])
    return weighted / denominator[..., None]


def on_device(prompt_x, decode_x, w_query, w_keyval, w_out, prompt_blocks, prompt_row):
    tp_count = lax.axis_size("tp")
    pool_count = lax.axis_size("pool")
    tp_index = lax.axis_index("tp")
    pool_index = lax.axis_index("pool")
    half_tokens = prompt_x.shape[0]
    tokens_here = half_tokens // tp_count
    blocks_here = tokens_here // BLK
    half_blocks = half_tokens // BLK
    total_blocks = half_blocks * pool_count
    keyval = lax.psum_scatter(
        jnp.dot(prompt_x, w_keyval, preferred_element_type=jnp.float32),
        "tp",
        scatter_dimension=0,
        tiled=True,
    )
    blocked = keyval.reshape(blocks_here, BLK, KVH, 2, HD)
    scales = (jnp.max(jnp.abs(blocked), axis=(1, 4)) + 1e-06).astype(jnp.bfloat16)
    stored = (blocked / scales.astype(jnp.float32)[:, None, :, :, None]).astype(jnp.bfloat16)
    stored = stored.reshape(blocks_here, BLK, KVH, 2 * HD)
    slot_row_all = block_rows(prompt_blocks, prompt_row, total_blocks)
    row_half = decode_x.shape[1]
    owner_half = slot_row_all // row_half
    first_block = pool_index * half_blocks + tp_index * blocks_here
    mine_owner = lax.dynamic_slice_in_dim(owner_half, first_block, blocks_here, 0)
    dest_head = np.arange(tp_count) * KVH // tp_count
    by_head = stored.transpose(2, 0, 1, 3)[dest_head]
    scale_head = scales.transpose(1, 0, 2)[dest_head]
    to_half = mine_owner[None, :] == jnp.arange(pool_count, dtype=jnp.int32)[:, None]
    zero_value = jnp.zeros((), jnp.bfloat16)
    send_vals = jnp.where(to_half[None, :, :, None, None], by_head[:, None], zero_value)
    send_scale = jnp.where(to_half[None, :, :, None], scale_head[:, None], zero_value)
    got_vals, got_scale = (
        lax.all_to_all(
            lax.all_to_all(send_vals, "tp", split_axis=0, concat_axis=0, tiled=True),
            "pool",
            split_axis=1,
            concat_axis=1,
            tiled=True,
        ),
        lax.all_to_all(
            lax.all_to_all(send_scale, "tp", split_axis=0, concat_axis=0, tiled=True),
            "pool",
            split_axis=1,
            concat_axis=1,
            tiled=True,
        ),
    )
    got_vals = got_vals.reshape(total_blocks, BLK, 2 * HD)
    got_scale = got_scale.reshape(total_blocks, 2)
    slot_row = (
        slot_row_all.reshape(pool_count, tp_count, blocks_here)
        .transpose(1, 0, 2)
        .reshape(total_blocks)
    )
    gathered = lax.all_gather(decode_x, "tp", axis=2, tiled=True)
    step_count, row_count, model_width = gathered.shape
    heads_here = w_query.shape[1] // HD
    queries = jnp.einsum("srd,de->sre", gathered, w_query, preferred_element_type=jnp.float32)
    queries = queries.astype(jnp.bfloat16).reshape(step_count, row_count, heads_here, HD)
    partial_new = jnp.einsum("srd,de->sre", decode_x, w_keyval, preferred_element_type=jnp.float32)
    summed_new = lax.psum(partial_new, "tp")
    fresh_keyval = summed_new.astype(jnp.bfloat16).reshape(step_count, row_count, KVH, 2 * HD)
    my_head = tp_index * KVH // tp_count
    fresh_keyval = lax.dynamic_index_in_dim(fresh_keyval, my_head, 2, keepdims=False)
    row_ids = pool_index * row_count + jnp.arange(row_count, dtype=jnp.int32)
    weighted = attend(queries, got_vals, got_scale, slot_row, fresh_keyval, row_ids)
    attended = weighted.reshape(step_count, row_count, heads_here * HD).astype(jnp.bfloat16)
    out_term = jnp.einsum("sre,ed->srd", attended, w_out, preferred_element_type=jnp.float32)
    return lax.psum_scatter(out_term, "tp", scatter_dimension=2, tiled=True).astype(jnp.bfloat16)


def solution(mesh):
    placed = (
        P(("group", "pool"), "tp"),
        P(None, ("group", "pool"), "tp"),
        P(None, "tp"),
        P("tp", None),
        P("tp", None),
        P("group"),
        P("group"),
    )
    return jax.shard_map(
        on_device,
        mesh=mesh,
        in_specs=placed,
        out_specs=P(None, ("group", "pool"), "tp"),
        check_vma=False,
    )
```

profile of v0, /device:TPU:0, one launch (start us, length us, event | category | flops | bytes accessed | tf_op | source)
XLA Modules:
  0.0 254.8 jit_solution(7903377930404320485)
XLA Ops:
  6.5 1.6 copy-done
  8.1 6.8 %fusion.50 = f32[1024,2048]{1,0:T(8,128)} fusion(bf16[1024,512]{1,0:T(8,128)(2,1)} %param.10, bf16[512,2048]{1,0:T(8,128)(2,1)S(1)} %copy-done), kind=kOutput, calls=%fused_computation.76 | convolution fusion | flops 2147483648 | bytes 11534336 | tf_op jit(solution)/shard_map/dot_general | solution.py:56
  15.0 0.7 all-gather.2.cloned.1.call-update
  15.8 0.5 fusion.4
  16.3 74.8 %all-reduce.1 = bf16[4,16,2048]{2,1,0:T(8,128)(2,1)S(1)} all-reduce(f32[4,16,2048]{2,1,0:T(8,128)S(1)} %fusion.4), channel_id=1, replica_groups=mesh['group'=2,'tp'=16,'pool'=1] {'tp'}, use_global_device_ids=true, to_apply=%region_6.7 | all-reduce | flops 131072 | bytes 786432 | tf_op jit(solution)/shard_map/psum | solution.py:106
  91.8 32.1 %reduce-scatter.3.cloned.1.call-done = f32[64,2048]{1,0:T(8,128)} async-done(((f32[1024,2048]{1,0:T(8,128)}), f32[64,2048]{1,0:T(8,128)}) %reduce-scatter.3.cloned.1.call-update) | async-done | bytes 524304 | tf_op jit(solution)/shard_map/reduce_scatter | solution.py:55
  123.8 1.9 abs.6
  125.8 1.5 abs.7
  128.3 0.6 gather_fusion
  128.9 0.6 gather_fusion.1
  129.7 0.7 copy.98
  130.4 4.3 %all-to-all-start.1 = ((bf16[16,1,4,2]{2,3,1,0:T(2,128)(2,1)}), bf16[16,1,4,2]{2,3,1,0:T(2,128)(2,1)S(1)}, u32[]{:S(2)}, u32[]{:S(2)}) async-start(bf16[16,1,4,2]{2,3,1,0:T(2,128)(2,1)} %copy.98), calls=%async_computation.2 | async-start | bytes 16384 | tf_op jit(solution)/shard_map/all_to_all | solution.py:86
  134.7 0.9 fusion.26
  135.6 5.5 %all-to-all-done.1 = bf16[16,1,4,2]{2,3,1,0:T(2,128)(2,1)S(1)} async-done(((bf16[16,1,4,2]{2,3,1,0:T(2,128)(2,1)}), bf16[16,1,4,2]{2,3,1,0:T(2,128)(2,1)S(1)}, u32[]{:S(2)}, u32[]{:S(2)}) %all-to-all-start.1) | async-done | bytes 288 | tf_op jit(solution)/shard_map/all_to_all | solution.py:86
  141.1 3.6 %all-to-all-start = ((bf16[16,1,4,16,256]{4,3,2,1,0:T(8,128)(2,1)}), bf16[16,1,4,16,256]{4,3,2,1,0:T(8,128)(2,1)S(1)}, u32[]{:S(2)}, u32[]{:S(2)}) async-start(bf16[16,1,4,16,256]{4,3,2,1,0:T(8,128)(2,1)} %fusion.26), calls=%async_computation.1 | async-start | bytes 1048576 | tf_op jit(solution)/shard_map/all_to_all | solution.py:79
  144.8 20.9 %all-gather.2.cloned.1.call-done = bf16[4,16,8192]{2,1,0:T(8,128)(2,1)} async-done(((bf16[4,16,512]{2,1,0:T(8,128)(2,1)}), bf16[4,16,8192]{2,1,0:T(8,128)(2,1)}) %all-gather.2.cloned.1.call-update) | async-done | bytes 1048592 | tf_op jit(solution)/shard_map/all_gather | solution.py:100
  165.7 5.3 %fusion.15 = bf16[4,16,512]{2,1,0:T(8,128)(2,1)S(1)} fusion(bf16[4,16,8192]{2,1,0:T(8,128)(2,1)} %all-gather.2.cloned.1.call-done, bf16[8192,512]{1,0:T(8,128)(2,1)} %param.12), kind=kOutput, calls=%fused_computation.20 | convolution fusion | flops 536903680 | bytes 9502720 | tf_op jit(solution)/shard_map/srd,de->sre/dot_general | solution.py:103
  171.0 0.7 fusion.49
  172.2 1.9 fusion.6
  174.6 2.2 fusion.7
  176.9 2.3 fusion.18
  179.2 6.3 %fusion = f32[4,16,8192]{2,1,0:T(8,128)} fusion(bf16[512,8192]{1,0:T(8,128)(2,1)} %param.14, bf16[4,4,2,8,128]{4,3,2,1,0:T(8,128)(2,1)S(1)} %fusion.18), kind=kOutput, calls=%fused_computation.2 | convolution fusion | flops 536870912 | bytes 10551296 | tf_op jit(solution)/shard_map/sre,ed->srd/dot_general | solution.py:113
  185.6 61.2 %reduce-scatter.5.cloned.1.call-done = f32[4,16,512]{2,1,0:T(8,128)} async-done(((f32[4,16,8192]{2,1,0:T(8,128)}), f32[4,16,512]{2,1,0:T(8,128)}) %reduce-scatter.5.cloned.1.call-update) | async-done | bytes 131088 | tf_op jit(solution)/shard_map/reduce_scatter | solution.py:114
  246.8 1.5 convert_element_type.67
  (54 shorter events, 3.2 us)
Async XLA Ops:
  6.5 1.6 copy-start
  6.5 117.3 %reduce-scatter.3.cloned.1.call-start = ((), (), s32[]{:S(2)}) async-start(), calls=%async_computation.5 | async-start | bytes 8912896 | tf_op jit(solution)/shard_map/reduce_scatter | solution.py:55
  14.9 0.8 copy-start.2
  14.9 150.7 %all-gather.2.cloned.1.call-start = ((), (), s32[]{:S(2)}) async-start(), calls=%async_computation.4 | async-start | bytes 1114112 | tf_op jit(solution)/shard_map/all_gather | solution.py:100
  15.7 75.5 %copy-start.3 = (s32[16]{0:T(128)S(1)}, s32[16]{0:T(128)}, u32[]{:S(2)}) copy-start(s32[16]{0:T(128)} %param.15) | copy-start | bytes 196
  15.8 75.8 %copy-start.5 = (s32[16]{0:T(128)S(1)}, s32[16]{0:T(128)}, u32[]{:S(2)}) copy-start(s32[16]{0:T(128)} %param.16) | copy-start | bytes 196
  15.8 76.0 %copy-start.4 = (s32[16]{0:T(128)S(1)}, s32[16]{0:T(128)}, u32[]{:S(2)}) copy-start(s32[16]{0:T(128)} %constant.66) | copy-start | bytes 196
  123.8 4.0 %copy-start.1 = (f32[64,2048]{1,0:T(8,128)S(1)}, f32[64,2048]{1,0:T(8,128)}, u32[]{:S(2)}) copy-start(f32[64,2048]{1,0:T(8,128)} %reduce-scatter.3.cloned.1.call-done) | copy-start | bytes 1572868
  130.4 10.8 %all-to-all-start.1 = ((bf16[16,1,4,2]{2,3,1,0:T(2,128)(2,1)}), bf16[16,1,4,2]{2,3,1,0:T(2,128)(2,1)S(1)}, u32[]{:S(2)}, u32[]{:S(2)}) async-start(bf16[16,1,4,2]{2,3,1,0:T(2,128)(2,1)} %copy.98), calls=%async_computation.2 | async-start | bytes 16384 | tf_op jit(solution)/shard_map/all_to_all | solution.py:86
  141.1 31.0 %all-to-all-start = ((bf16[16,1,4,16,256]{4,3,2,1,0:T(8,128)(2,1)}), bf16[16,1,4,16,256]{4,3,2,1,0:T(8,128)(2,1)S(1)}, u32[]{:S(2)}, u32[]{:S(2)}) async-start(bf16[16,1,4,16,256]{4,3,2,1,0:T(8,128)(2,1)} %fusion.26), calls=%async_computation.1 | async-start | bytes 1048576 | tf_op jit(solution)/shard_map/all_to_all | solution.py:79
  144.7 102.1 %reduce-scatter.5.cloned.1.call-start = ((), (), s32[]{:S(2)}) async-start(), calls=%async_computation.6 | async-start | bytes 2228224 | tf_op jit(solution)/shard_map/reduce_scatter | solution.py:114
Sparse Core Ops, SparseCore 0:
  15.1 108.7 reduce-scatter.2
  126.0 39.6 all-gather.1
  185.7 61.0 reduce-scatter.4
where the time goes:
time: 255 us
  waiting for transfers between devices  120 us (47%)
  blocking collectives  74.8 us (29%)
  matrix products  24 us (9%)
  between operations  13.3 us (5%)
  starting transfers between devices  7.99 us (3%)
  other arithmetic  7.65 us (3%)
  local copies, waits for them, and re-layouts  6.69 us (3%)
    psum x1, blocking collectives, on_device(): summed_new = lax.psum(partial_new, 'tp')  74.8 us
    reduce_scatter x1, waiting for transfers between devices, on_device(): lax.psum_scatter(out_term, 'tp', scatter_dimension=2, tiled=True)  61.2 us
    reduce_scatter x1, waiting for transfers between devices, on_device(): lax.psum_scatter(jnp.dot(prompt_x, w_keyval, preferred_element_type=jnp.f...  32.1 us
    all_gather x1, waiting for transfers between devices, on_device(): gathered = lax.all_gather(decode_x, 'tp', axis=2, tiled=True)  20.9 us
    dot_general x1, matrix products, on_device(): jnp.dot(prompt_x, w_keyval, preferred_element_type=jnp.float32)  6.79 us
    dot_general x1, matrix products, on_device(): jnp.einsum('sre,ed->srd', attended, w_out, preferred_element_type=jnp.flo...  6.33 us
    all_to_all x1, waiting for transfers between devices, on_device(): lax.all_to_all(send_scale, 'tp', split_axis=0, concat_axis=0, tiled=True)  5.52 us
    dot_general x1, matrix products, on_device(): jnp.einsum('srd,de->sre', gathered, w_query, preferred_element_type=jnp.f...  5.27 us
  transfers between devices with their start and end apart: 5, of which 4 were waited for; matrix products, arithmetic and copies ran while one was open for 6% of the time, Pallas kernels for 0%

commit v1 on v0

--- a/solution.py
+++ b/solution.py
@@ -103,7 +103,8 @@
     queries = jnp.einsum("srd,de->sre", gathered, w_query, preferred_element_type=jnp.float32)
     queries = queries.astype(jnp.bfloat16).reshape(step_count, row_count, heads_here, HD)
     partial_new = jnp.einsum("srd,de->sre", decode_x, w_keyval, preferred_element_type=jnp.float32)
-    summed_new = lax.psum(partial_new, "tp")
+    _detail_joints = lambda x_local: jnp.sum(lax.all_gather(x_local, axis_name="tp"), axis=0)
+    summed_new = _detail_joints(partial_new)
     fresh_keyval = summed_new.astype(jnp.bfloat16).reshape(step_count, row_count, KVH, 2 * HD)
     my_head = tp_index * KVH // tp_count
     fresh_keyval = lax.dynamic_index_in_dim(fresh_keyval, my_head, 2, keepdims=False)

time: 255 us -> 323 us (1.27)
  waiting for transfers between devices: 120 us -> 259 us
  blocking collectives: 74.8 us -> 0 us
  other arithmetic: 7.65 us -> 11.9 us
    psum x1 -> x0, blocking collectives: 74.8 us -> none  [on_device(): summed_new = lax.psum(partial_new, 'tp')]
    reduce_scatter x1, waiting for transfers between devices: 32.1 us -> 104 us  [on_device(): lax.psum_scatter(jnp.dot(prompt_x, w_keyval, preferred_element_type=jnp.f...]
    all_gather x0 -> x1, waiting for transfers between devices: none -> 68 us  [on_device(): lax.all_gather(x_local, axis_name='tp')]
    reduce_sum x0 -> x1, other arithmetic: none -> 3.96 us  [on_device(): jnp.sum(lax.all_gather(x_local, axis_name='tp'), axis=0)]
  transfers between devices with their start and end apart: 5 -> 6, of which waited for: 4 -> 5; matrix products, arithmetic and copies ran while one was open for 6% -> 5% of each run, Pallas kernels for 0% -> 0%
where the time goes in v1:
time: 323 us; the launch traced here: 322 us
  waiting for transfers between devices  259 us (80%)
  matrix products  23.3 us (7%)
  between operations  13.3 us (4%)
  other arithmetic  11.9 us (4%)
  starting transfers between devices  8.05 us (2%)
  local copies, waits for them, and re-layouts  6.66 us (2%)
    reduce_scatter x1, waiting for transfers between devices, on_device(): lax.psum_scatter(jnp.dot(prompt_x, w_keyval, preferred_element_type=jnp.f...  104 us
    all_gather x1, waiting for transfers between devices, on_device(): lax.all_gather(x_local, axis_name='tp')  68 us
    reduce_scatter x1, waiting for transfers between devices, on_device(): lax.psum_scatter(out_term, 'tp', scatter_dimension=2, tiled=True)  60.5 us
    all_gather x1, waiting for transfers between devices, on_device(): gathered = lax.all_gather(decode_x, 'tp', axis=2, tiled=True)  20.9 us
    dot_general x1, matrix products, on_device(): jnp.dot(prompt_x, w_keyval, preferred_element_type=jnp.float32)  6.77 us
  transfers between devices with their start and end apart: 6, of which 5 were waited for; matrix products, arithmetic and copies ran while one was open for 5% of the time, Pallas kernels for 0%

profile of v1, /device:TPU:0, one launch (start us, length us, event | category | flops | bytes accessed | tf_op | source)
XLA Modules:
  0.0 322.4 jit_solution(2951061519129435480)
XLA Ops:
  6.5 1.6 copy-done
  8.1 6.8 %fusion.50 = f32[1024,2048]{1,0:T(8,128)} fusion(bf16[1024,512]{1,0:T(8,128)(2,1)} %param.10, bf16[512,2048]{1,0:T(8,128)(2,1)S(1)} %copy-done), kind=kOutput, calls=%fused_computation.76 | convolution fusion | flops 2147483648 | bytes 11534336 | tf_op jit(solution)/shard_map/dot_general | solution.py:56
  15.0 0.7 all-gather.4.cloned.1.call-update
  15.8 1.3 fusion.4
  17.7 103.6 %reduce-scatter.3.cloned.1.call-done = f32[64,2048]{1,0:T(8,128)} async-done(((f32[1024,2048]{1,0:T(8,128)}), f32[64,2048]{1,0:T(8,128)}) %reduce-scatter.3.cloned.1.call-update) | async-done | bytes 524304 | tf_op jit(solution)/shard_map/reduce_scatter | solution.py:55
  121.3 2.0 abs.6
  123.3 1.5 abs.7
  126.4 0.6 gather_fusion.1
  127.1 0.7 copy.97
  127.8 4.4 %all-to-all-start.1 = ((bf16[16,1,4,2]{2,3,1,0:T(2,128)(2,1)}), bf16[16,1,4,2]{2,3,1,0:T(2,128)(2,1)S(1)}, u32[]{:S(2)}, u32[]{:S(2)}) async-start(bf16[16,1,4,2]{2,3,1,0:T(2,128)(2,1)} %copy.97), calls=%async_computation.2 | async-start | bytes 16384 | tf_op jit(solution)/shard_map/all_to_all | solution.py:86
  132.2 1.0 fusion.26
  133.2 5.4 %all-to-all-done.1 = bf16[16,1,4,2]{2,3,1,0:T(2,128)(2,1)S(1)} async-done(((bf16[16,1,4,2]{2,3,1,0:T(2,128)(2,1)}), bf16[16,1,4,2]{2,3,1,0:T(2,128)(2,1)S(1)}, u32[]{:S(2)}, u32[]{:S(2)}) %all-to-all-start.1) | async-done | bytes 288 | tf_op jit(solution)/shard_map/all_to_all | solution.py:86
  138.6 3.6 %all-to-all-start = ((bf16[16,1,4,16,256]{4,3,2,1,0:T(8,128)(2,1)}), bf16[16,1,4,16,256]{4,3,2,1,0:T(8,128)(2,1)S(1)}, u32[]{:S(2)}, u32[]{:S(2)}) async-start(bf16[16,1,4,16,256]{4,3,2,1,0:T(8,128)(2,1)} %fusion.26), calls=%async_computation.1 | async-start | bytes 1048576 | tf_op jit(solution)/shard_map/all_to_all | solution.py:79
  142.2 20.9 %all-gather.4.cloned.1.call-done = bf16[4,16,8192]{2,1,0:T(8,128)(2,1)} async-done(((bf16[4,16,512]{2,1,0:T(8,128)(2,1)}), bf16[4,16,8192]{2,1,0:T(8,128)(2,1)}) %all-gather.4.cloned.1.call-update) | async-done | bytes 1048592 | tf_op jit(solution)/shard_map/all_gather | solution.py:100
  163.1 5.3 %fusion.15 = bf16[4,16,512]{2,1,0:T(8,128)(2,1)S(1)} fusion(bf16[4,16,8192]{2,1,0:T(8,128)(2,1)} %all-gather.4.cloned.1.call-done, bf16[8192,512]{1,0:T(8,128)(2,1)} %param.12), kind=kOutput, calls=%fused_computation.20 | convolution fusion | flops 536903680 | bytes 9502720 | tf_op jit(solution)/shard_map/srd,de->sre/dot_general | solution.py:103
  168.8 1.9 fusion.6
  170.8 68.0 %all-gather.6.cloned.1.call-done = f32[64,16,2048]{2,1,0:T(8,128)} async-done(((f32[4,16,2048]{2,1,0:T(8,128)}), f32[64,16,2048]{2,1,0:T(8,128)}) %all-gather.6.cloned.1.call-update) | async-done | bytes 8388624 | tf_op jit(solution)/shard_map/all_gather | solution.py:106
  238.8 4.0 %reduce_sum.47 = bf16[4,16,2048]{2,1,0:T(8,128)(2,1)S(1)} reduce(f32[16,4,16,2048]{3,2,1,0:T(8,128)} %bitcast.97, f32[]{:T(128)} %constant.62.clone.1), dimensions={0}, to_apply=%region_6.7 | reduce | flops 1966080 | bytes 8650756 | tf_op jit(solution)/shard_map/reduce_sum | solution.py:106
  242.9 0.7 fusion.49
  244.3 2.4 fusion.7
  246.7 0.7 fusion.18
  247.4 6.3 %fusion = f32[4,16,8192]{2,1,0:T(8,128)} fusion(bf16[512,8192]{1,0:T(8,128)(2,1)} %param.14, bf16[4,4,2,8,128]{4,3,2,1,0:T(8,128)(2,1)S(1)} %fusion.18), kind=kOutput, calls=%fused_computation.2 | convolution fusion | flops 536870912 | bytes 10551296 | tf_op jit(solution)/shard_map/sre,ed->srd/dot_general | solution.py:114
  253.8 60.5 %reduce-scatter.5.cloned.1.call-done = f32[4,16,512]{2,1,0:T(8,128)} async-done(((f32[4,16,8192]{2,1,0:T(8,128)}), f32[4,16,512]{2,1,0:T(8,128)}) %reduce-scatter.5.cloned.1.call-update) | async-done | bytes 131088 | tf_op jit(solution)/shard_map/reduce_scatter | solution.py:115
  314.3 1.5 convert_element_type.72
  (59 shorter events, 3.8 us)
Async XLA Ops:
  6.5 1.6 copy-start
  6.5 114.7 %reduce-scatter.3.cloned.1.call-start = ((), (), s32[]{:S(2)}) async-start(), calls=%async_computation.5 | async-start | bytes 8912896 | tf_op jit(solution)/shard_map/reduce_scatter | solution.py:55
  14.9 0.9 copy-start.3
  14.9 2.2 copy-start.4
  14.9 2.5 copy-start.6
  15.0 2.7 copy-start.5
  15.0 148.2 %all-gather.4.cloned.1.call-start = ((), (), s32[]{:S(2)}) async-start(), calls=%async_computation.4 | async-start | bytes 1114112 | tf_op jit(solution)/shard_map/all_gather | solution.py:100
  15.7 223.0 %all-gather.6.cloned.1.call-start = ((), (), s32[]{:S(2)}) async-start(), calls=%async_computation.7 | async-start | bytes 8912896 | tf_op jit(solution)/shard_map/all_gather | solution.py:106
  121.3 4.1 %copy-start.2 = (f32[64,2048]{1,0:T(8,128)S(1)}, f32[64,2048]{1,0:T(8,128)}, u32[]{:S(2)}) copy-start(f32[64,2048]{1,0:T(8,128)} %reduce-scatter.3.cloned.1.call-done) | copy-start | bytes 1572868
  127.8 10.7 %all-to-all-start.1 = ((bf16[16,1,4,2]{2,3,1,0:T(2,128)(2,1)}), bf16[16,1,4,2]{2,3,1,0:T(2,128)(2,1)S(1)}, u32[]{:S(2)}, u32[]{:S(2)}) async-start(bf16[16,1,4,2]{2,3,1,0:T(2,128)(2,1)} %copy.97), calls=%async_computation.2 | async-start | bytes 16384 | tf_op jit(solution)/shard_map/all_to_all | solution.py:86
  138.6 30.2 %all-to-all-start = ((bf16[16,1,4,16,256]{4,3,2,1,0:T(8,128)(2,1)}), bf16[16,1,4,16,256]{4,3,2,1,0:T(8,128)(2,1)S(1)}, u32[]{:S(2)}, u32[]{:S(2)}) async-start(bf16[16,1,4,16,256]{4,3,2,1,0:T(8,128)(2,1)} %fusion.26), calls=%async_computation.1 | async-start | bytes 1048576 | tf_op jit(solution)/shard_map/all_to_all | solution.py:79
  142.1 172.1 %reduce-scatter.5.cloned.1.call-start = ((), (), s32[]{:S(2)}) async-start(), calls=%async_computation.6 | async-start | bytes 2228224 | tf_op jit(solution)/shard_map/reduce_scatter | solution.py:115
  244.3 2.4 copy-start.1
Sparse Core Ops, SparseCore 0:
  15.0 106.1 reduce-scatter.2
  123.4 39.6 all-gather.3
  165.3 73.4 all-gather.5
  253.9 60.3 reduce-scatter.4
